TPU v7x, 32 devices: a whole 2x2x4 slice. The times are simulated.
32 devices in a mesh: dp: 16 (over z, y, x), tensor: 2 (over core).
Axes of the slice: x: 2, y: 2, z: 4, core: 2. Of those that a mesh axis runs over, the one named last changes fastest.
Arguments:
- layer_in: bfloat16 [8192, 768], P(('dp', 'tensor')), may hold values from -6 to 6
- norm1_gain: bfloat16 [768], P('tensor'), may hold values from 0.5 to 1.5
- qkv_weight: bfloat16 [768, 2304], P('tensor'), may hold values from -0.21875 to 0.21875
- out_weight: bfloat16 [768, 768], P('tensor'), may hold values from -4 to 4
- norm2_gain: bfloat16 [768], P('tensor'), may hold values from 0.5 to 1.5
- mlp_weight: bfloat16 [3, 768, 1152], P(None, None, 'tensor'), may hold values from -0.21875 to 0.21875
- cotangent: bfloat16 [8192, 768], P(('dp', 'tensor')), may hold values from -6 to 6
Outputs:
- layer_out: bfloat16 [8192, 768], P(('dp', 'tensor'))
- input_grad: float32 [8192, 768], P(('dp', 'tensor'))
- norm1_grad: float32 [768], P('tensor')
- qkv_grad: float32 [768, 2304], P('tensor')
- out_grad: float32 [768, 768], P('tensor')
- norm2_grad: float32 [768], P('tensor')
- mlp_grad: float32 [3, 768, 1152], P(None, None, 'tensor')
All inputs are finite; a program needn't handle non-finite values.
Results may differ from a plain program's by a relative error of at most 0.023.
Values may be sent and summed in bfloat16 or wider, within the bound.
A program may use at most 128 MiB of HBM per device.

v0:
```python
import jax
import jax.numpy as jnp
from jax import lax
from jax.sharding import PartitionSpec as P

HEADS = 12
HEAD_DIM = 64
SEQ = 512
EPS = 1e-05
THETA = 160000.0


def swapped(value, axis, distance):
    mask = 2**distance
    pairs = [(source, source ^ mask) for source in range(lax.axis_size(axis))]
    return lax.ppermute(value, axis, pairs)


def rope_tables(positions):
    half = HEAD_DIM // 2
    freq = THETA ** (-jnp.arange(half).astype(jnp.float32) * 2.0 / HEAD_DIM)
    angle = positions.astype(jnp.float32)[:, None] * freq[None, :]
    return (jnp.cos(angle)[:, None, :], jnp.sin(angle)[:, None, :])


def rotate(values, cosine, sine):
    half = HEAD_DIM // 2
    first, second = (values[..., :half], values[..., half:])
    return jnp.concatenate([first * cosine - second * sine, second * cosine + first * sine], -1)


def unrotate(values, cosine, sine):
    half = HEAD_DIM // 2
    first, second = (values[..., :half], values[..., half:])
    return jnp.concatenate([first * cosine + second * sine, second * cosine - first * sine], -1)


def layer_norm_forward(values, gain):
    centred = values - jnp.mean(values, -1, keepdims=True)
    inverse = lax.rsqrt(jnp.mean(centred * centred, -1, keepdims=True) + EPS)
    normed = centred * inverse
    return (normed * gain, normed, inverse)


def layer_norm_backward(upstream, normed, inverse, gain):
    scaled = upstream * gain
    back = inverse * (
        scaled
        - jnp.mean(scaled, -1, keepdims=True)
        - normed * jnp.mean(scaled * normed, -1, keepdims=True)
    )
    return (back, jnp.sum(upstream * normed, 0))


def gelu_parts(values):
    cdf = 0.5 * (1.0 + jax.scipy.special.erf(values * 0.7071067811865476))
    density = jnp.exp(-0.5 * values * values) * 0.3989422804014327
    return (values * cdf, cdf + values * density)


def right_product(left, weight):
    return lax.dot_general(
        left, weight, (((1,), (1,)), ((), ())), preferred_element_type=jnp.float32
    )


def left_product(left, right):
    return lax.dot_general(
        left, right, (((0,), (0,)), ((), ())), preferred_element_type=jnp.float32
    )


def collect_keys(key_own, value_own, position_slot):
    pair = (key_own, value_own)
    far_key, far_value = swapped((pair[0], pair[1]), "tensor", 0)
    upper = (position_slot >> 0) % 2 == 1
    pair = (
        jnp.where(
            upper, jnp.concatenate([far_key, pair[0]], 0), jnp.concatenate([pair[0], far_key], 0)
        ),
        jnp.where(
            upper,
            jnp.concatenate([far_value, pair[1]], 0),
            jnp.concatenate([pair[1], far_value], 0),
        ),
    )
    return pair


def return_grads(key_grad, value_grad, position_slot):
    pair = (key_grad, value_grad)
    middle = pair[0].shape[0] // 2
    upper = (position_slot >> 0) % 2 == 1
    keep_key = jnp.where(upper, pair[0][middle:], pair[0][:middle])
    send_key = jnp.where(upper, pair[0][:middle], pair[0][middle:])
    keep_value = jnp.where(upper, pair[1][middle:], pair[1][:middle])
    send_value = jnp.where(upper, pair[1][:middle], pair[1][middle:])
    back_key = swapped(send_key.astype(jnp.bfloat16), "tensor", 0).astype(send_key.dtype)
    back_value = swapped(send_value.astype(jnp.bfloat16), "tensor", 0).astype(send_value.dtype)
    pair = (keep_key + back_key, keep_value + back_value)
    return pair


def body(layer_in, norm1_gain, qkv_weight, out_weight, norm2_gain, mlp_weight, cotangent):
    f32 = jnp.float32
    bf16 = jnp.bfloat16
    rows = layer_in.shape[0]
    width = layer_in.shape[1]
    span = SEQ // rows
    scale = HEAD_DIM ** (-0.5)
    first_norm_gain, second_norm_gain, w_qkv, w_out = (
        lax.all_gather(norm1_gain, "tensor", axis=0, tiled=True),
        lax.all_gather(norm2_gain, "tensor", axis=0, tiled=True),
        lax.all_gather(qkv_weight, "tensor", axis=0, tiled=True),
        lax.all_gather(out_weight, "tensor", axis=0, tiled=True),
    )
    first_norm_gain = first_norm_gain.astype(f32)
    second_norm_gain = second_norm_gain.astype(f32)
    position_slot = lax.axis_index("tensor") % span
    cosine, sine = rope_tables(position_slot * rows + jnp.arange(rows, dtype=jnp.int32))
    input_float_rows = layer_in.astype(f32)
    first_normed_rows, standardized_first, inverse_deviation_first = layer_norm_forward(
        input_float_rows, first_norm_gain
    )
    h1 = first_normed_rows.astype(bf16)
    qkv = jnp.dot(h1, w_qkv, preferred_element_type=f32)
    query = rotate(qkv[:, :width].reshape(rows, HEADS, HEAD_DIM), cosine, sine).astype(bf16)
    key_own = (
        rotate(qkv[:, width : 2 * width].reshape(rows, HEADS, HEAD_DIM), cosine, sine)
        .astype(bf16)
        .reshape(rows, width)
    )
    value_own = qkv[:, 2 * width :].astype(bf16)
    key_all, value_all = collect_keys(key_own, value_own, position_slot)
    keys = key_all.reshape(SEQ, HEADS, HEAD_DIM)
    values = value_all.reshape(SEQ, HEADS, HEAD_DIM)
    scores = jnp.einsum("qhd,khd->hqk", query, keys, preferred_element_type=f32) * scale
    total = jnp.log(jnp.sum(jnp.exp(scores), -1))
    probs_b = jnp.exp(scores - total[..., None]).astype(bf16)
    attended = (
        jnp.einsum("hqk,khd->qhd", probs_b, values, preferred_element_type=f32)
        .astype(bf16)
        .reshape(rows, width)
    )
    attention_mixed = input_float_rows + jnp.dot(attended, w_out, preferred_element_type=f32)
    second_normed_rows, standardized_second, inverse_deviation_second = layer_norm_forward(
        attention_mixed, second_norm_gain
    )
    h2 = second_normed_rows.astype(bf16)
    dz_f = cotangent.astype(f32)
    group = lax.all_gather(h2, "tensor", axis=0, tiled=True)
    gate_pre = jnp.dot(group, mlp_weight[0], preferred_element_type=f32)
    up_pre = jnp.dot(group, mlp_weight[1], preferred_element_type=f32)
    gel, slope = gelu_parts(gate_pre)
    hidden = (gel * up_pre).astype(bf16)
    branch = lax.psum_scatter(
        right_product(hidden, mlp_weight[2]).astype(jnp.bfloat16),
        "tensor",
        scatter_dimension=0,
        tiled=True,
    ).astype(jnp.float32)
    layer_out = (attention_mixed + branch).astype(bf16)
    grad_group = lax.all_gather(cotangent, "tensor", axis=0, tiled=True)
    grad_hidden = jnp.dot(grad_group, mlp_weight[2], preferred_element_type=f32)
    grad_gate = (grad_hidden * up_pre * slope).astype(bf16)
    grad_up = (grad_hidden * gel).astype(bf16)
    grad_mlp = jnp.stack(
        [
            left_product(group, grad_gate),
            left_product(group, grad_up),
            left_product(grad_group, hidden),
        ]
    )
    gradient_hidden_second = lax.psum_scatter(
        right_product(grad_gate, mlp_weight[0]) + right_product(grad_up, mlp_weight[1]),
        "tensor",
        scatter_dimension=0,
        tiled=True,
    )
    second_norm_backward, gradient_gain_second = layer_norm_backward(
        gradient_hidden_second, standardized_second, inverse_deviation_second, second_norm_gain
    )
    grad_mixed = dz_f + second_norm_backward
    grad_mixed_b = grad_mixed.astype(bf16)
    grad_wout = left_product(attended, grad_mixed_b)
    grad_att = right_product(grad_mixed_b, w_out).astype(bf16).reshape(rows, HEADS, HEAD_DIM)
    scores = jnp.einsum("qhd,khd->hqk", query, keys, preferred_element_type=f32) * scale
    probs = jnp.exp(scores - total[..., None])
    probs_b = probs.astype(bf16)
    grad_probs = jnp.einsum("qhd,khd->hqk", grad_att, values, preferred_element_type=f32)
    delta = jnp.einsum(
        "qhd,qhd->hq", grad_att.astype(f32), attended.reshape(rows, HEADS, HEAD_DIM).astype(f32)
    )
    grad_scores = (probs * (grad_probs - delta[..., None])).astype(bf16)
    grad_query = jnp.einsum("hqk,khd->qhd", grad_scores, keys, preferred_element_type=f32) * scale
    grad_keys = jnp.einsum("hqk,qhd->khd", grad_scores, query, preferred_element_type=f32) * scale
    grad_values = jnp.einsum("hqk,qhd->khd", probs_b, grad_att, preferred_element_type=f32)
    key_total, value_total = return_grads(
        grad_keys.reshape(SEQ, width), grad_values.reshape(SEQ, width), position_slot
    )
    grad_q = unrotate(grad_query, cosine, sine).reshape(rows, width)
    grad_k = unrotate(key_total.reshape(rows, HEADS, HEAD_DIM), cosine, sine).reshape(rows, width)
    grad_qkv = jnp.concatenate([grad_q, grad_k, value_total], 1).astype(bf16)
    grad_wqkv = left_product(h1, grad_qkv)
    gradient_hidden_first = right_product(grad_qkv, w_qkv)
    first_norm_backward, gradient_gain_first = layer_norm_backward(
        gradient_hidden_first, standardized_first, inverse_deviation_first, first_norm_gain
    )
    input_grad = grad_mixed + first_norm_backward
    shares = (
        lax.psum_scatter(
            grad_wqkv.astype(jnp.bfloat16), "tensor", scatter_dimension=0, tiled=True
        ).astype(jnp.float32),
        lax.psum_scatter(
            grad_wout.astype(jnp.bfloat16), "tensor", scatter_dimension=0, tiled=True
        ).astype(jnp.float32),
        lax.psum_scatter(
            gradient_gain_first.astype(jnp.bfloat16), "tensor", scatter_dimension=0, tiled=True
        ).astype(jnp.float32),
        lax.psum_scatter(
            gradient_gain_second.astype(jnp.bfloat16), "tensor", scatter_dimension=0, tiled=True
        ).astype(jnp.float32),
    )
    totals = (
        lax.psum(shares[0].astype(jnp.bfloat16), "dp").astype(jnp.float32),
        lax.psum(shares[1].astype(jnp.bfloat16), "dp").astype(jnp.float32),
        lax.psum(shares[2].astype(jnp.bfloat16), "dp").astype(jnp.float32),
        lax.psum(shares[3].astype(jnp.bfloat16), "dp").astype(jnp.float32),
        lax.psum(grad_mlp.astype(jnp.bfloat16), "dp").astype(jnp.float32),
    )
    return (layer_out, input_grad, totals[2], totals[0], totals[1], totals[3], totals[4])


def solution(mesh):
    return jax.shard_map(
        body,
        mesh=mesh,
        in_specs=(
            P(("dp", "tensor"), None),
            P("tensor"),
            P("tensor", None),
            P("tensor", None),
            P("tensor"),
            P(None, None, "tensor"),
            P(("dp", "tensor"), None),
        ),
        out_specs=(
            P(("dp", "tensor"), None),
            P(("dp", "tensor"), None),
            P("tensor"),
            P("tensor", None),
            P("tensor", None),
            P("tensor"),
            P(None, None, "tensor"),
        ),
        check_vma=False,
    )
```

profile of v0, /device:TPU:0, one launch (start us, length us, event | category | flops | bytes accessed | tf_op | source)
XLA Modules:
  0.0 339.7 jit_solution(17604484921782706955)
XLA Ops:
  8.8 2.0 all-gather
  11.3 1.8 all-gather.1
  14.0 11.1 %all-gather.5.cloned.1.call-done = bf16[768,2304]{1,0:T(8,128)(2,1)} async-done(((bf16[384,2304]{1,0:T(8,128)(2,1)}), bf16[768,2304]{1,0:T(8,128)(2,1)}) %all-gather.5.cloned.1.call-update) | async-done | bytes 3538960 | tf_op jit(solution)/shard_map/all_gather | solution.py:114
  25.0 3.1 fusion.89
  29.4 1.4 copy.32
  33.2 2.5 all_gather.23
  37.3 1.3 copy.29
  38.6 4.9 %fusion.71 = f32[12,256,512]{2,1,0:T(8,128)} fusion(bf16[256,12,32]{0,2,1:T(8,128)(2,1)S(1)} %get-tuple-element.32, bf16[256,12,32]{0,2,1:T(8,128)(2,1)S(1)} %get-tuple-element.31, bf16[256,12,64]{0,2,1:T(8,128)(2,1)S(1)} %maximum_convert_fusion, bf16[256,12,64]{0,2,1:T(8,128)(2,1)} %bitcast.7, pred[]{:T(512)S(6)} %eq.8), kind=kOutput, calls=%fused_computation.109 | convolution fusion | flops 205651968 | bytes 7471105 | tf_op jit(solution)/shard_map/qhd,khd->hqk/dot_general | solution.py:137
  43.6 7.0 %fusion.18 = bf16[12,64,256]{2,1,0:T(8,128)(2,1)S(1)} fusion(f32[12,256,512]{2,1,0:T(8,128)} %fusion.71, bf16[256,12,64]{0,2,1:T(8,128)(2,1)S(1)} %bitcast.91, bf16[256,12,64]{0,2,1:T(8,128)(2,1)S(1)} %bitcast.93, pred[]{:T(512)S(6)} %eq.8), kind=kOutput, calls=%fused_computation.29 | convolution fusion | flops 211357184 | bytes 7471105 | tf_op jit(solution)/shard_map/hqk,khd->qhd/dot_general | solution.py:141
  50.6 1.9 fusion.92
  52.9 2.5 all_gather.22
  59.4 2.0 convolution_add_fusion
  61.5 2.9 convolution_convert_fusion.5
  64.6 7.2 %fusion.1 = f32[12,256,512]{2,1,0:T(8,128)} fusion(bf16[256,12,32]{0,2,1:T(8,128)(2,1)S(1)} %get-tuple-element.32, bf16[256,12,32]{0,2,1:T(8,128)(2,1)S(1)} %get-tuple-element.31, bf16[256,12,64]{0,2,1:T(8,128)(2,1)S(1)} %maximum_convert_fusion, bf16[256,12,64]{0,2,1:T(8,128)(2,1)} %bitcast.7, pred[]{:T(512)S(6)} %eq.8), kind=kOutput, calls=%fused_computation.2 | convolution fusion | flops 416026112 | bytes 7471105 | tf_op jit(solution)/shard_map/reduce_sum | solution.py:138
  71.8 2.2 multiply_reduce_fusion
  74.6 9.4 %reduce-scatter.5.cloned.1.call-done = bf16[256,768]{1,0:T(8,128)(2,1)} async-done(((bf16[512,768]{1,0:T(8,128)(2,1)}), bf16[256,768]{1,0:T(8,128)(2,1)}) %reduce-scatter.5.cloned.1.call-update) | async-done | bytes 393232 | tf_op jit(solution)/shard_map/reduce_scatter | solution.py:156
  83.9 2.1 multiply_add_fusion
  86.0 1.5 convolution_convert_fusion.1
  88.6 8.0 %fusion.11 = f32[512,12,64]{0,2,1:T(8,128)} fusion(bf16[256,12,64]{0,2,1:T(8,128)(2,1)S(1)} %bitcast.84, f32[12,256,512]{2,1,0:T(8,128)} %fusion.71), kind=kOutput, calls=%fused_computation.18 | convolution fusion | flops 207621632 | bytes 8257536 | tf_op jit(solution)/shard_map/hqk,qhd->khd/dot_general | solution.py:197
  96.7 4.6 %multiply_convert_fusion = bf16[12,256,512]{2,1,0:T(8,128)(2,1)S(1)} fusion(f32[12,256,512]{2,1,0:T(8,128)} %fusion.1, f32[12,256]{1,0:T(8,128)S(1)} %fusion.59, bf16[256,12,64]{0,2,1:T(8,128)(2,1)} %bitcast.86, bf16[256,12,64]{0,2,1:T(8,128)(2,1)} %bitcast.92, bf16[256,12,64]{0,2,1:T(8,128)(2,1)} %bitcast.94, pred[]{:T(512)S(6)} %eq.8), kind=kOutput, calls=%fused_computation.3 | convolution fusion | flops 209584128 | bytes 10629121 | tf_op jit(solution)/shard_map/qhd,khd->hqk/dot_general | solution.py:190
  104.2 1.6 slice_select_fusion.1
  107.1 2.2 fusion.17
  111.7 3.1 convolution_convert_fusion
  115.9 1.7 fusion.14
  119.3 1.8 pad_maximum_fusion
  121.1 8.7 %reduce-scatter.9.cloned.1.call-done = bf16[384,2304]{1,0:T(8,128)(2,1)} async-done(((bf16[768,2304]{1,0:T(8,128)(2,1)}), bf16[384,2304]{1,0:T(8,128)(2,1)}) %reduce-scatter.9.cloned.1.call-update) | async-done | bytes 1769488 | tf_op jit(solution)/shard_map/reduce_scatter | solution.py:211
  131.7 3.4 %fusion.56 = (bf16[768]{0:T(1024)(128)(2,1)S(1)}, f32[256]{0:T(256)S(1)}, f32[256]{0:T(256)S(1)}, f32[256,768]{1,0:T(8,128)S(1)}) fusion(bf16[256,768]{1,0:T(8,128)(2,1)S(1)} %copy-done.2, f32[256]{0:T(256)S(1)} %copy-done.36, f32[256]{0:T(256)S(1)} %broadcast_multiply_fusion.5, f32[768]{0:T(1024)S(1)} %reshape.182, ...), kind=kOutput, calls=%fused_computation.64 | convolution fusion | flops 911276800 | bytes 5906944 | tf_op jit(solution)/shard_map/dot_general | solution.py:62
  135.2 2.5 all-reduce.4
  137.8 44.4 %all-reduce.2 = (bf16[384]{0:T(512)(128)(2,1)S(1)}, bf16[384]{0:T(512)(128)(2,1)S(1)}) all-reduce(bf16[384]{0:T(512)(128)(2,1)S(1)} %dynamic-slice.1, bf16[384]{0:T(512)(128)(2,1)S(1)} %dynamic-slice.3), channel_id=1, replica_groups=mesh['dp'=16,'tensor'=2] {'dp'}, use_global_device_ids=true, to_apply=%region_13.14 | all-reduce | flops 768 | bytes 3072 | tf_op jit(solution)/shard_map/psum | solution.py:227
  184.6 140.7 %all-reduce.7.cloned.1.call-done = (bf16[384,2304]{1,0:T(8,128)(2,1)}, bf16[384,768]{1,0:T(8,128)(2,1)}, bf16[3,768,576]{1,2,0:T(8,128)(2,1)}) async-done(((bf16[384,2304]{1,0:T(8,128)(2,1)}, bf16[384,768]{1,0:T(8,128)(2,1)}, bf16[3,768,576]{1,2,0:T(8,128)(2,1)}), (bf16[384,2304]{1,0:T(8,128)(2,1)}, bf16[384,768]{1,0:T(8,128)(2,1)}, bf16[3,768,576]{1,2,0:T(8,128)(2,1)})) %all-reduce.7.cloned.1.call-update) | async-done | bytes 5013520 | tf_op jit(solution)/shard_map/psum | solution.py:225
  325.3 3.6 %convert_element_type.167 = f32[384,2304]{1,0:T(8,128)} convert(bf16[384,2304]{1,0:T(8,128)(2,1)} %get-tuple-element.15) | non-fusion elementwise | flops 884736 | bytes 5308416 | tf_op jit(solution)/shard_map/convert_element_type | solution.py:225
  330.0 2.8 convert_element_type.172
  (165 shorter events, 28.5 us)
Async XLA Ops:
  7.2 3.6 %copy-start.2 = (bf16[256,768]{1,0:T(8,128)(2,1)S(1)}, bf16[256,768]{1,0:T(8,128)(2,1)}, u32[]{:S(2)}) copy-start(bf16[256,768]{1,0:T(8,128)(2,1)} %param.7) | copy-start | bytes 1179652
  7.2 4.1 %copy-start.39 = (bf16[384]{0:T(512)(128)(2,1)S(1)}, bf16[384]{0:T(512)(128)(2,1)}, u32[]{:S(2)}) copy-start(bf16[384]{0:T(512)(128)(2,1)} %param.11) | copy-start | bytes 2308
  7.2 17.8 %all-gather.5.cloned.1.call-start = ((), (), s32[]{:S(2)}) async-start(), calls=%async_computation.4 | async-start | bytes 5308416 | tf_op jit(solution)/shard_map/all_gather | solution.py:114
  7.9 42.7 %all-gather.7.cloned.1.call-start = ((), (), s32[]{:S(2)}) async-start(), calls=%async_computation.5 | async-start | bytes 1769472 | tf_op jit(solution)/shard_map/all_gather | solution.py:115
  8.7 63.1 %reduce-scatter.7.cloned.1.call-start = ((), (), s32[]{:S(2)}) async-start(), calls=%async_computation.7 | async-start | bytes 2359296 | tf_op jit(solution)/shard_map/reduce_scatter | solution.py:174
  11.2 17.0 %copy-start.35 = (f32[256]{0:T(256)}, f32[256]{0:T(256)S(1)}, u32[]{:S(2)}) copy-start(f32[256]{0:T(256)S(1)} %add_rsqrt_fusion.1) | copy-start | bytes 3076
  31.8 5.1 %copy-start.10 = (f32[256,768]{1,0:T(8,128)S(1)}, f32[256,768]{1,0:T(8,128)}, u32[]{:S(2)}) copy-start(f32[256,768]{1,0:T(8,128)} %get-tuple-element.24) | copy-start | bytes 2359300
  32.6 32.0 %copy-start.19 = (bf16[256,12,64]{0,2,1:T(8,128)(2,1)}, bf16[256,12,64]{0,2,1:T(8,128)(2,1)S(1)}, u32[]{:S(2)}) copy-start(bf16[256,12,64]{0,2,1:T(8,128)(2,1)S(1)} %maximum_convert_fusion) | copy-start | bytes 1179652
  32.6 4.6 %copy-start.28 = (f32[256,32]{0,1:T(8,128)S(1)}, f32[256,32]{0,1:T(8,128)}, u32[]{:S(2)}) copy-start(f32[256,32]{0,1:T(8,128)} %get-tuple-element.37) | copy-start | bytes 98308
  32.6 4.6 %copy-start.30 = (f32[256,32]{0,1:T(8,128)S(1)}, f32[256,32]{0,1:T(8,128)}, u32[]{:S(2)}) copy-start(f32[256,32]{0,1:T(8,128)} %get-tuple-element.38) | copy-start | bytes 98308
  32.6 6.0 %collective-permute-start.1 = (bf16[256,768]{0,1:T(8,128)(2,1)S(1)}, bf16[256,768]{0,1:T(8,128)(2,1)}, u32[]{:S(2)}, u32[]{:S(2)}) collective-permute-start(bf16[256,768]{0,1:T(8,128)(2,1)S(1)} %bitcast.90), channel_id=1, source_target_pairs={{0,1},{1,0},{2,3},{3,2},{4,5},{5,4},{6,7},{7,6},{8,9},{9,8},{10,11... | collective-permute-start | bytes 1179656 | tf_op jit(solution)/shard_map/ppermute | solution.py:16
  32.9 4.4 %collective-permute-start = (bf16[256,768]{1,0:T(8,128)(2,1)}, bf16[256,768]{1,0:T(8,128)(2,1)}, u32[]{:S(2)}, u32[]{:S(2)}) collective-permute-start(bf16[256,768]{1,0:T(8,128)(2,1)} %slice.148), channel_id=1, source_target_pairs={{0,1},{1,0},{2,3},{3,2},{4,5},{5,4},{6,7},{7,6},{8,9},{9,8},{10,11... | collective-permute-start | bytes 1179656 | tf_op jit(solution)/shard_map/ppermute | solution.py:16
  36.9 6.7 %copy-start.21 = (bf16[256,768]{0,1:T(8,128)(2,1)}, bf16[256,768]{0,1:T(8,128)(2,1)S(1)}, u32[]{:S(2)}) copy-start(bf16[256,768]{0,1:T(8,128)(2,1)S(1)} %copy.30) | copy-start | bytes 1179652
  37.3 27.3 %copy-start.13 = (bf16[256,12,32]{0,2,1:T(8,128)(2,1)}, bf16[256,12,32]{0,2,1:T(8,128)(2,1)S(1)}, u32[]{:S(2)}) copy-start(bf16[256,12,32]{0,2,1:T(8,128)(2,1)S(1)} %get-tuple-element.31) | copy-start | bytes 589828
  37.3 27.3 %copy-start.15 = (bf16[256,12,32]{0,2,1:T(8,128)(2,1)}, bf16[256,12,32]{0,2,1:T(8,128)(2,1)S(1)}, u32[]{:S(2)}) copy-start(bf16[256,12,32]{0,2,1:T(8,128)(2,1)S(1)} %get-tuple-element.32) | copy-start | bytes 589828
  38.6 5.0 %copy-start.22 = (bf16[256,768]{0,1:T(8,128)(2,1)}, bf16[256,768]{0,1:T(8,128)(2,1)S(1)}, u32[]{:S(2)}) copy-start(bf16[256,768]{0,1:T(8,128)(2,1)S(1)} %copy.29) | copy-start | bytes 1179652
  52.7 3.4 copy-start.34
  61.4 22.5 %reduce-scatter.5.cloned.1.call-start = ((), (), s32[]{:S(2)}) async-start(), calls=%async_computation.6 | async-start | bytes 1179648 | tf_op jit(solution)/shard_map/reduce_scatter | solution.py:156
  64.3 56.8 %reduce-scatter.11.cloned.1.call-start = ((), (), s32[]{:S(2)}) async-start(), calls=%async_computation.9 | async-start | bytes 1769472 | tf_op jit(solution)/shard_map/reduce_scatter | solution.py:214
  71.8 12.1 %copy-start.18 = (bf16[256,768]{1,0:T(8,128)(2,1)S(1)}, bf16[256,768]{1,0:T(8,128)(2,1)}, u32[]{:S(2)}) copy-start(bf16[256,768]{1,0:T(8,128)(2,1)} %param.13) | copy-start | bytes 1179652
  71.8 12.1 %copy-start.9 = (f32[256,768]{1,0:T(8,128)S(1)}, f32[256,768]{1,0:T(8,128)}, u32[]{:S(2)}) copy-start(f32[256,768]{1,0:T(8,128)} %reduce-scatter.7.cloned.1.call-done) | copy-start | bytes 2359300
  88.6 8.0 %copy-start.8 = (bf16[256,768]{0,1:T(8,128)(2,1)}, bf16[256,768]{0,1:T(8,128)(2,1)S(1)}, u32[]{:S(2)}) copy-start(bf16[256,768]{0,1:T(8,128)(2,1)S(1)} %copy.33) | copy-start | bytes 1179652
  96.7 4.6 %copy-start.14 = (bf16[256,12,32]{0,2,1:T(8,128)(2,1)S(1)}, bf16[256,12,32]{0,2,1:T(8,128)(2,1)}, u32[]{:S(2)}) copy-start(bf16[256,12,32]{0,2,1:T(8,128)(2,1)} %copy-done.13) | copy-start | bytes 589828
  96.7 4.6 %copy-start.16 = (bf16[256,12,32]{0,2,1:T(8,128)(2,1)S(1)}, bf16[256,12,32]{0,2,1:T(8,128)(2,1)}, u32[]{:S(2)}) copy-start(bf16[256,12,32]{0,2,1:T(8,128)(2,1)} %copy-done.15) | copy-start | bytes 589828
  104.0 5.4 %collective-permute-start.2 = (bf16[256,768]{0,1:T(8,128)(2,1)}, bf16[256,768]{0,1:T(8,128)(2,1)}, u32[]{:S(2)}, u32[]{:S(2)}) collective-permute-start(bf16[256,768]{0,1:T(8,128)(2,1)} %bitcast.21), channel_id=1, source_target_pairs={{0,1},{1,0},{2,3},{3,2},{4,5},{5,4},{6,7},{7,6},{8,9},{9,8},{10,11... | collective-permute-start | bytes 1179656 | tf_op jit(solution)/shard_map/ppermute | solution.py:16
  104.2 25.6 %reduce-scatter.9.cloned.1.call-start = ((), (), s32[]{:S(2)}) async-start(), calls=%async_computation.8 | async-start | bytes 5308416 | tf_op jit(solution)/shard_map/reduce_scatter | solution.py:211
  106.3 4.5 %collective-permute-start.3 = (bf16[256,768]{0,1:T(8,128)(2,1)S(1)}, bf16[256,768]{0,1:T(8,128)(2,1)S(1)}, u32[]{:S(2)}, u32[]{:S(2)}) collective-permute-start(bf16[256,768]{0,1:T(8,128)(2,1)S(1)} %bitcast.99), channel_id=1, source_target_pairs={{0,1},{1,0},{2,3},{3,2},{4,5},{5,4},{6,7},{7,6},{8,9},{9,8},{10,11... | collective-permute-start | bytes 1179656 | tf_op jit(solution)/shard_map/ppermute | solution.py:16
  114.8 210.4 %all-reduce.7.cloned.1.call-start = ((), (), s32[]{:S(2)}) async-start(), calls=%async_computation.10 | async-start | bytes 10027008 | tf_op jit(solution)/shard_map/psum | solution.py:225
  131.7 3.4 %copy-start.37 = (bf16[768]{0:T(1024)(128)(2,1)S(1)}, bf16[768]{0:T(1024)(128)(2,1)}, u32[]{:S(2)}) copy-start(bf16[768]{0:T(1024)(128)(2,1)} %get-tuple-element.7) | copy-start | bytes 4612
  131.7 51.7 %copy-start.1 = (f32[256,768]{1,0:T(8,128)S(1)}, f32[256,768]{1,0:T(8,128)}, u32[]{:S(2)}) copy-start(f32[256,768]{1,0:T(8,128)} %copy-done) | copy-start | bytes 2359300
  325.3 3.7 %copy-start.27 = (bf16[384,768]{1,0:T(8,128)(2,1)S(1)}, bf16[384,768]{1,0:T(8,128)(2,1)}, u32[]{:S(2)}) copy-start(bf16[384,768]{1,0:T(8,128)(2,1)} %get-tuple-element.16) | copy-start | bytes 1769476
  325.3 4.7 %copy-start.12 = (bf16[3,768,576]{1,2,0:T(8,128)(2,1)S(1)}, bf16[3,768,576]{1,2,0:T(8,128)(2,1)}, u32[]{:S(2)}) copy-start(bf16[3,768,576]{1,2,0:T(8,128)(2,1)} %get-tuple-element.17) | copy-start | bytes 7962628
  (23 other events, 38.2 us)
Sparse Core Ops, SparseCore 0:
  9.5 15.4 all-gather.4
  26.5 10.4 all-gather.6
  61.5 10.2 reduce-scatter.6
  74.4 9.4 reduce-scatter.4
  104.3 9.7 reduce-scatter.10
  116.8 12.9 reduce-scatter.8
  136.7 188.5 all-reduce.6
where the time goes:
time: 341 us; the launch traced here: 340 us
  waiting for transfers between devices  171 us (50%)
  matrix products  59 us (17%)
  blocking collectives  55.7 us (16%)
  other arithmetic  23.5 us (7%)
  between operations  15.6 us (5%)
  local copies, waits for them, and re-layouts  12.8 us (4%)
    psum x1, waiting for transfers between devices, body(): lax.psum(shares[0].astype(jnp.bfloat16), 'dp').astype(jnp.float32)  141 us
    psum x1, blocking collectives, body(): lax.psum(shares[2].astype(jnp.bfloat16), 'dp').astype(jnp.float32)  44.4 us
    all_gather x1, waiting for transfers between devices, body(): lax.all_gather(qkv_weight, 'tensor', axis=0, tiled=True)  11.1 us
    dot_general x5, matrix products, right_product(): lax.dot_general(left, weight, (((1,), (1,)), ((), ())), preferred_element...  9.54 us
    reduce_scatter x1, waiting for transfers between devices, body(): lax.psum_scatter(right_product(hidden, mlp_weight[2]).astype(jnp.bfloat16...  9.36 us
    reduce_scatter x1, waiting for transfers between devices, body(): lax.psum_scatter(grad_wqkv.astype(jnp.bfloat16), 'tensor', scatter_dimens...  8.69 us
    dot_general x1, matrix products, body(): jnp.einsum('hqk,qhd->khd', probs_b, grad_att, preferred_element_type=f32)  7.95 us
    dot_general x5, matrix products, left_product(): lax.dot_general(left, right, (((0,), (0,)), ((), ())), preferred_element_...  7.5 us
  transfers between devices with their start and end apart: 11, of which 4 were waited for; matrix products, arithmetic and copies ran while one was open for 17% of the time, Pallas kernels for 0%

commit v1 on v0

--- a/solution.py
+++ b/solution.py
@@ -8,6 +8,11 @@
 SEQ = 512
 EPS = 1e-05
 THETA = 160000.0
+
+
+def add_all(value, axis):
+    parts = lax.all_gather(value, axis)
+    return jnp.sum(parts, axis=0)
 
 
 def swapped(value, axis, distance):
@@ -222,7 +227,7 @@
         ).astype(jnp.float32),
     )
     totals = (
-        lax.psum(shares[0].astype(jnp.bfloat16), "dp").astype(jnp.float32),
+        add_all(shares[0].astype(jnp.bfloat16), "dp").astype(jnp.float32),
         lax.psum(shares[1].astype(jnp.bfloat16), "dp").astype(jnp.float32),
         lax.psum(shares[2].astype(jnp.bfloat16), "dp").astype(jnp.float32),
         lax.psum(shares[3].astype(jnp.bfloat16), "dp").astype(jnp.float32),

time: 341 us -> 611 us (1.79)
  waiting for transfers between devices: 171 us -> 431 us
  other arithmetic: 23.5 us -> 35.2 us
    all_gather x0 -> x1, waiting for transfers between devices: none -> 295 us  [add_all(): parts = lax.all_gather(value, axis)]
    psum x1, waiting for transfers between devices: 141 us -> 104 us  [body(): lax.psum(shares[1].astype(jnp.bfloat16), 'dp').astype(jnp.float32)]
    reduce_sum x0 -> x1, other arithmetic: none -> 10.2 us  [add_all(): return jnp.sum(parts, axis=0)]
  transfers between devices with their start and end apart: 11 -> 12, of which waited for: 4 -> 5; matrix products, arithmetic and copies ran while one was open for 17% -> 10% of each run, Pallas kernels for 0% -> 0%
where the time goes in v1:
time: 611 us
  waiting for transfers between devices  431 us (71%)
  matrix products  60.3 us (10%)
  blocking collectives  54.8 us (9%)
  other arithmetic  35.2 us (6%)
  between operations  15.5 us (3%)
  local copies, waits for them, and re-layouts  12.1 us (2%)
    all_gather x1, waiting for transfers between devices, add_all(): parts = lax.all_gather(value, axis)  295 us
    psum x1, waiting for transfers between devices, body(): lax.psum(shares[1].astype(jnp.bfloat16), 'dp').astype(jnp.float32)  104 us
    psum x1, blocking collectives, body(): lax.psum(shares[2].astype(jnp.bfloat16), 'dp').astype(jnp.float32)  43.7 us
  transfers between devices with their start and end apart: 12, of which 5 were waited for; matrix products, arithmetic and copies ran while one was open for 10% of the time, Pallas kernels for 0%

profile of v1, /device:TPU:0, one launch (start us, length us, event | category | flops | bytes accessed | tf_op | source)
XLA Modules:
  0.0 610.6 jit_solution(4019420231046960083)
XLA Ops:
  8.8 2.0 all-gather.1
  11.3 1.8 all-gather.2
  14.0 11.1 %all-gather.7.cloned.1.call-done = bf16[768,2304]{1,0:T(8,128)(2,1)} async-done(((bf16[384,2304]{1,0:T(8,128)(2,1)}), bf16[768,2304]{1,0:T(8,128)(2,1)}) %all-gather.7.cloned.1.call-update) | async-done | bytes 3538960 | tf_op jit(solution)/shard_map/all_gather | solution.py:119
  25.0 3.1 fusion.89
  33.2 2.5 all_gather.29
  38.6 4.9 fusion.71
  43.6 7.0 %fusion.18 = bf16[12,64,256]{2,1,0:T(8,128)(2,1)S(1)} fusion(f32[12,256,512]{2,1,0:T(8,128)} %fusion.71, bf16[256,12,64]{0,2,1:T(8,128)(2,1)S(1)} %bitcast.93, bf16[256,12,64]{0,2,1:T(8,128)(2,1)S(1)} %bitcast.95, pred[]{:T(512)S(6)} %eq.8), kind=kOutput, calls=%fused_computation.29 | convolution fusion | flops 211357184 | bytes 7471105 | tf_op jit(solution)/shard_map/hqk,khd->qhd/dot_general | solution.py:146
  50.6 2.0 fusion.92
  53.4 2.4 all_gather.28
  57.3 2.0 multiply_convert_fusion.1
  61.0 2.0 convolution_add_fusion
  63.0 3.1 convolution_convert_fusion.5
  66.4 7.2 %fusion.1 = f32[12,256,512]{2,1,0:T(8,128)} fusion(bf16[256,12,32]{0,2,1:T(8,128)(2,1)S(1)} %get-tuple-element.31, bf16[256,12,32]{0,2,1:T(8,128)(2,1)S(1)} %get-tuple-element.30, bf16[256,12,64]{0,2,1:T(8,128)(2,1)S(1)} %copy-done.17, bf16[256,12,64]{0,2,1:T(8,128)(2,1)} %bitcast.7, pred[]{:T(512)S(6)} %eq.8), kind=kOutput, calls=%fused_computation.2 | convolution fusion | flops 416026112 | bytes 7471105 | tf_op jit(solution)/shard_map/reduce_sum | solution.py:143
  73.6 2.1 multiply_reduce_fusion
  76.3 9.2 %reduce-scatter.5.cloned.1.call-done = bf16[256,768]{1,0:T(8,128)(2,1)} async-done(((bf16[512,768]{1,0:T(8,128)(2,1)}), bf16[256,768]{1,0:T(8,128)(2,1)}) %reduce-scatter.5.cloned.1.call-update) | async-done | bytes 393232 | tf_op jit(solution)/shard_map/reduce_scatter | solution.py:161
  85.5 2.5 multiply_add_fusion
  90.2 8.0 %fusion.11 = f32[512,12,64]{0,2,1:T(8,128)} fusion(bf16[256,12,64]{0,2,1:T(8,128)(2,1)S(1)} %bitcast.86, f32[12,256,512]{2,1,0:T(8,128)} %fusion.71), kind=kOutput, calls=%fused_computation.18 | convolution fusion | flops 207621632 | bytes 8257536 | tf_op jit(solution)/shard_map/hqk,qhd->khd/dot_general | solution.py:202
  98.3 4.6 multiply_convert_fusion
  108.7 2.2 fusion.17
  113.3 3.1 convolution_convert_fusion
  117.6 1.7 fusion.14
  120.6 1.8 pad_maximum_fusion
  122.5 8.9 %reduce-scatter.9.cloned.1.call-done = bf16[384,2304]{1,0:T(8,128)(2,1)} async-done(((bf16[768,2304]{1,0:T(8,128)(2,1)}), bf16[384,2304]{1,0:T(8,128)(2,1)}) %reduce-scatter.9.cloned.1.call-update) | async-done | bytes 1769488 | tf_op jit(solution)/shard_map/reduce_scatter | solution.py:216
  132.7 3.4 fusion.56
  136.1 2.5 all-reduce.4
  138.8 43.7 %all-reduce.2 = (bf16[384]{0:T(512)(128)(2,1)S(1)}, bf16[384]{0:T(512)(128)(2,1)S(1)}) all-reduce(bf16[384]{0:T(512)(128)(2,1)S(1)} %dynamic-slice.1, bf16[384]{0:T(512)(128)(2,1)S(1)} %dynamic-slice.3), channel_id=1, replica_groups=mesh['dp'=16,'tensor'=2] {'dp'}, use_global_device_ids=true, to_apply=%region_13.14 | all-reduce | flops 768 | bytes 3072 | tf_op jit(solution)/shard_map/psum | solution.py:232
  184.8 104.5 %all-reduce.7.cloned.1.call-done = (bf16[384,768]{1,0:T(8,128)(2,1)}, bf16[3,768,576]{1,2,0:T(8,128)(2,1)}) async-done(((bf16[384,768]{1,0:T(8,128)(2,1)}, bf16[3,768,576]{1,2,0:T(8,128)(2,1)}), (bf16[384,768]{1,0:T(8,128)(2,1)}, bf16[3,768,576]{1,2,0:T(8,128)(2,1)})) %all-reduce.7.cloned.1.call-update) | async-done | bytes 3244048 | tf_op jit(solution)/shard_map/psum | solution.py:231
  289.3 2.2 convert_element_type.171
  291.5 4.6 convert_element_type.174
  296.1 295.5 %all-gather.11.cloned.1.call-done = bf16[6144,2304]{1,0:T(8,128)(2,1)} async-done(((bf16[384,2304]{1,0:T(8,128)(2,1)}), bf16[6144,2304]{1,0:T(8,128)(2,1)}) %all-gather.11.cloned.1.call-update) | async-done | bytes 28311568 | tf_op jit(solution)/shard_map/all_gather | solution.py:14
  591.5 10.2 %reduce_sum.121 = bf16[384,2304]{1,0:T(8,128)(2,1)S(1)} reduce(bf16[16,384,2304]{2,1,0:T(8,128)(2,1)} %bitcast.83, bf16[]{:T(256)} %constant.63.clone.1), dimensions={0}, to_apply=%region_15.16 | reduce | flops 13271040 | bytes 30081026 | tf_op jit(solution)/shard_map/reduce_sum | solution.py:15
  601.7 2.0 convert_element_type.169
  (163 shorter events, 31.4 us)
Async XLA Ops:
  7.2 4.1 copy-start.37
  7.2 17.8 %all-gather.7.cloned.1.call-start = ((), (), s32[]{:S(2)}) async-start(), calls=%async_computation.4 | async-start | bytes 5308416 | tf_op jit(solution)/shard_map/all_gather | solution.py:119
  7.9 42.7 %all-gather.9.cloned.1.call-start = ((), (), s32[]{:S(2)}) async-start(), calls=%async_computation.5 | async-start | bytes 1769472 | tf_op jit(solution)/shard_map/all_gather | solution.py:120
  8.7 65.0 %reduce-scatter.7.cloned.1.call-start = ((), (), s32[]{:S(2)}) async-start(), calls=%async_computation.7 | async-start | bytes 2359296 | tf_op jit(solution)/shard_map/reduce_scatter | solution.py:179
  11.2 17.0 %copy-start.33 = (f32[256]{0:T(256)}, f32[256]{0:T(256)S(1)}, u32[]{:S(2)}) copy-start(f32[256]{0:T(256)S(1)} %add_rsqrt_fusion.1) | copy-start | bytes 3076
  31.8 5.1 copy-start.9
  32.6 4.6 copy-start.25
  32.6 4.6 copy-start.27
  32.6 6.0 copy-start.16
  32.6 6.0 collective-permute-start.1
  32.9 4.4 collective-permute-start
  36.8 6.7 %copy-start.19 = (bf16[256,768]{0,1:T(8,128)(2,1)}, bf16[256,768]{0,1:T(8,128)(2,1)S(1)}, u32[]{:S(2)}) copy-start(bf16[256,768]{0,1:T(8,128)(2,1)S(1)} %copy.30) | copy-start | bytes 1179652
  37.3 29.1 %copy-start.11 = (bf16[256,12,32]{0,2,1:T(8,128)(2,1)}, bf16[256,12,32]{0,2,1:T(8,128)(2,1)S(1)}, u32[]{:S(2)}) copy-start(bf16[256,12,32]{0,2,1:T(8,128)(2,1)S(1)} %get-tuple-element.30) | copy-start | bytes 589828
  37.3 29.1 %copy-start.13 = (bf16[256,12,32]{0,2,1:T(8,128)(2,1)}, bf16[256,12,32]{0,2,1:T(8,128)(2,1)S(1)}, u32[]{:S(2)}) copy-start(bf16[256,12,32]{0,2,1:T(8,128)(2,1)S(1)} %get-tuple-element.31) | copy-start | bytes 589828
  38.6 5.0 copy-start.20
  50.6 5.2 copy-start.10
  63.0 22.5 %reduce-scatter.5.cloned.1.call-start = ((), (), s32[]{:S(2)}) async-start(), calls=%async_computation.6 | async-start | bytes 1179648 | tf_op jit(solution)/shard_map/reduce_scatter | solution.py:161
  66.1 7.5 %copy-start.32 = (f32[256]{0:T(256)S(1)}, f32[256]{0:T(256)}, u32[]{:S(2)}) copy-start(f32[256]{0:T(256)} %copy-done.31) | copy-start | bytes 3076
  66.1 56.3 %reduce-scatter.11.cloned.1.call-start = ((), (), s32[]{:S(2)}) async-start(), calls=%async_computation.9 | async-start | bytes 1769472 | tf_op jit(solution)/shard_map/reduce_scatter | solution.py:219
  90.2 8.0 %copy-start.8 = (bf16[256,768]{0,1:T(8,128)(2,1)}, bf16[256,768]{0,1:T(8,128)(2,1)S(1)}, u32[]{:S(2)}) copy-start(bf16[256,768]{0,1:T(8,128)(2,1)S(1)} %copy.33) | copy-start | bytes 1179652
  98.3 4.6 copy-start.12
  98.3 4.6 copy-start.14
  105.6 5.4 collective-permute-start.2
  105.8 25.6 %reduce-scatter.9.cloned.1.call-start = ((), (), s32[]{:S(2)}) async-start(), calls=%async_computation.8 | async-start | bytes 5308416 | tf_op jit(solution)/shard_map/reduce_scatter | solution.py:216
  107.9 4.2 copy-start.26
  107.9 4.2 copy-start.28
  107.9 4.5 collective-permute-start.3
  116.5 172.9 %all-reduce.7.cloned.1.call-start = ((), (), s32[]{:S(2)}) async-start(), calls=%async_computation.11 | async-start | bytes 6488064 | tf_op jit(solution)/shard_map/psum | solution.py:231
  122.4 9.0 %copy-start.40 = (u32[32]{0:T(128)S(1)}, u32[32]{0:T(128)}, u32[]{:S(2)}) copy-start(u32[32]{0:T(128)} %constant.67) | copy-start | bytes 388
  122.4 10.3 %copy-start.30 = (bf16[256,768]{0,1:T(8,128)(2,1)S(1)}, bf16[256,768]{0,1:T(8,128)(2,1)}, u32[]{:S(2)}) copy-start(bf16[256,768]{0,1:T(8,128)(2,1)} %copy-done.29) | copy-start | bytes 1179652
  122.4 469.1 %all-gather.11.cloned.1.call-start = ((), (), s32[]{:S(2)}) async-start(), calls=%async_computation.10 | async-start | bytes 30081024 | tf_op jit(solution)/shard_map/all_gather | solution.py:14
  132.7 51.0 %copy-start.1 = (f32[256,768]{1,0:T(8,128)S(1)}, f32[256,768]{1,0:T(8,128)}, u32[]{:S(2)}) copy-start(f32[256,768]{1,0:T(8,128)} %copy-done) | copy-start | bytes 2359300
  (21 other events, 41.3 us)
Sparse Core Ops, SparseCore 0:
  9.5 15.4 all-gather.6
  26.5 10.4 all-gather.8
  63.1 10.2 reduce-scatter.6
  76.0 9.4 reduce-scatter.4
  105.9 9.7 reduce-scatter.10
  118.4 12.9 reduce-scatter.8
  137.8 151.5 all-reduce.6
  292.1 299.3 all-gather.10
